TPU v7x, 32 devices: a whole 2x2x4 slice. The times are simulated.
32 devices in a mesh: row: 4 (over y, core), col: 8 (over z, x).
Axes of the slice: x: 2, y: 2, z: 4, core: 2. Of those that a mesh axis runs over, the one named last changes fastest.
Arguments:
- images: float32 [4, 128, 16384], P(None, 'row', 'col'), may hold values from -6 to 6
Outputs:
- coefficients: float32 [4, 128, 16384], P(None, 'row', 'col')
All inputs are finite; a program needn't handle non-finite values.
Results may differ from a plain program's by a relative error of at most 0.00002.
Values sent between devices are 32-bit elements; how exact they have to be, the bound alone decides.
A program may use at most 128 MiB of HBM per device.

v0:
```python
import jax
import jax.numpy as jnp
from jax import lax
from jax.sharding import PartitionSpec as P

LEVELS = 3


PREDICT_ONE = -1.586134342
UPDATE_ONE = -0.05298011854
PREDICT_TWO = 0.8829110762
UPDATE_TWO = 0.4435068522
SCALE_HIGH = 1.230174105
SCALE_LOW = 1.0 / 1.230174105


def with_halo(block, sides, width):
    for axis, dim in sides:
        count = lax.axis_size(axis)
        forward = [(i, i + 1) for i in range(count - 1)]
        backward = [(target, source) for source, target in forward]
        low = lax.ppermute(
            lax.slice_in_dim(block, block.shape[dim] - width, None, axis=dim), axis, forward
        )
        high = lax.ppermute(lax.slice_in_dim(block, 0, width, axis=dim), axis, backward)
        block = jnp.concatenate([low, block, high], axis=dim)
    return block


def segment(values, start, stop, along):
    return lax.slice_in_dim(values, start, stop, 1, along)


def lifting(extended, along):
    length = extended.shape[along]
    halves = length // 2
    evens = lax.slice_in_dim(extended, 0, length, 2, along)
    odds = lax.slice_in_dim(extended, 1, length, 2, along)
    predicted = segment(odds, 0, halves - 1, along) + PREDICT_ONE * (
        segment(evens, 0, halves - 1, along) + segment(evens, 1, halves, along)
    )
    updated = segment(evens, 1, halves - 1, along) + UPDATE_ONE * (
        segment(predicted, 0, halves - 2, along) + segment(predicted, 1, halves - 1, along)
    )
    refined = segment(predicted, 1, halves - 2, along) + PREDICT_TWO * (
        segment(updated, 0, halves - 3, along) + segment(updated, 1, halves - 2, along)
    )
    smoothed = segment(updated, 1, halves - 3, along) + UPDATE_TWO * (
        segment(refined, 0, halves - 4, along) + segment(refined, 1, halves - 3, along)
    )
    lowpass = smoothed * SCALE_LOW
    highpass = segment(refined, 1, halves - 3, along) * SCALE_HIGH
    paired = jnp.stack([lowpass, highpass], axis=along + 1)
    shape = list(extended.shape)
    shape[along] = length - 8
    return paired.reshape(shape)


def mirror(extended, along, at_start, at_end, margin):
    length = extended.shape[along]
    front = jnp.flip(segment(extended, margin + 1, 2 * margin + 1, along), along)
    behind = jnp.flip(segment(extended, length - 2 * margin - 1, length - margin - 1, along), along)
    head = jnp.where(at_start, front, segment(extended, 0, margin, along))
    tail = jnp.where(at_end, behind, segment(extended, length - margin, length, along))
    return jnp.concatenate(
        [head, segment(extended, margin, length - margin, along), tail], axis=along
    )


def shards(images):
    row_start = lax.axis_index("row") == 0
    row_end = lax.axis_index("row") == lax.axis_size("row") - 1
    col_start = lax.axis_index("col") == 0
    col_end = lax.axis_index("col") == lax.axis_size("col") - 1
    results = []
    lowband = images
    for level_index in range(LEVELS):
        extended = with_halo(lowband, (("row", 1), ("col", 2)), 4)
        extended = mirror(extended, 1, row_start, row_end, 4)
        extended = mirror(extended, 2, col_start, col_end, 4)
        vertical = lifting(extended, 1)
        transformed = lifting(vertical, 2)
        results.append(transformed)
        lowband = transformed[:, ::2, ::2]
    combined = results[-1]
    for transformed in reversed(results[:-1]):
        combined = transformed.at[:, ::2, ::2].set(combined)
    return combined


def solution(mesh):
    return jax.shard_map(
        shards,
        mesh=mesh,
        in_specs=(P(None, "row", "col"),),
        out_specs=P(None, "row", "col"),
        check_vma=False,
    )
```

profile of v0, /device:TPU:9, one launch (start us, length us, event | category | flops | bytes accessed | tf_op | source)
XLA Modules:
  0.0 305.7 jit_solution(14628329524991916664)
XLA Ops:
  1.2 3.7 %collective-permute-start = (f32[4,4,2048]{2,1,0:T(4,128)S(1)}, f32[4,4,2048]{2,1,0:T(4,128)S(1)}, u32[]{:S(2)}, u32[]{:S(2)}) collective-permute-start(f32[4,4,2048]{2,1,0:T(4,128)S(1)} %get-tuple-element.19), channel_id=1, source_target_pairs={{0,8},{8,16},{16,24},{1,9},{9,17},{17,25},{2,10},{10,18},{18,26},{... | collective-permute-start | bytes 393224 | tf_op jit(solution)/shard_map/ppermute | solution.py:22
  4.9 1.9 collective-permute-start.1
  9.1 2.1 collective-permute-done.1
  12.5 3.0 collective-permute-start.3
  15.5 2.3 collective-permute-start.2
  18.4 3.2 %collective-permute-done.2 = f32[4,40,4]{2,1,0:T(8,128)S(1)} collective-permute-done((f32[4,40,4]{2,1,0:T(8,128)S(1)}, f32[4,40,4]{2,1,0:T(8,128)S(1)}, u32[]{:S(2)}, u32[]{:S(2)}) %collective-permute-start.2) | collective-permute-done | bytes 2592 | tf_op jit(solution)/shard_map/ppermute | solution.py:22
  21.6 1.9 concatenate.43
  27.0 1.9 concatenate.45
  31.5 18.2 %slice.418 = f32[4,32,1028]{2,0,1:T(4,128)S(1)} slice(f32[4,32,2056]{2,0,1:T(4,128)S(1)} %bitcast.55), slice={[0:4:1], [0:32:1], [0:2056:2]} | slice | bytes 1052672 | tf_op jit(solution)/shard_map/slice | solution.py:37
  49.7 18.2 %slice.420 = f32[4,32,1028]{2,0,1:T(4,128)S(1)} slice(f32[4,32,2056]{2,0,1:T(4,128)S(1)} %bitcast.56), slice={[0:4:1], [0:32:1], [1:2056:2]} | slice | bytes 1052672 | tf_op jit(solution)/shard_map/slice | solution.py:38
  70.6 4.5 %copy.56 = f32[4,32,1024,2]{1,3,2,0:T(2,128)} copy(f32[4,32,1024,2]{2,0,1,3:T(4,128)S(1)} %pad_maximum_fusion.3) | data formatting | bytes 2097152 | tf_op jit(solution)/shard_map/stack | solution.py:53
  75.1 15.6 %slice.432 = f32[4,16,1024]{1,2,0:T(8,128)S(1)} slice(f32[4,32,2048]{1,2,0:T(8,128)} %bitcast.54), slice={[0:4:1], [0:32:2], [0:2048:2]} | slice | bytes 524288 | tf_op jit(solution)/shard_map/slice | solution.py:84
  90.8 2.6 fusion.74
  93.4 2.2 copy.57
  95.6 2.9 copy.58
  100.3 3.6 %collective-permute-start.4 = (f32[4,4,1024]{2,1,0:T(4,128)S(1)}, f32[4,4,1024]{2,1,0:T(4,128)}, u32[]{:S(2)}, u32[]{:S(2)}) collective-permute-start(f32[4,4,1024]{2,1,0:T(4,128)S(1)} %copy.57), channel_id=1, source_target_pairs={{0,8},{8,16},{16,24},{1,9},{9,17},{17,25},{2,10},{10,18},{18,26},{... | collective-permute-start | bytes 196616 | tf_op jit(solution)/shard_map/ppermute | solution.py:22
  106.3 1.9 collective-permute-start.7
  108.2 3.5 %collective-permute-start.6 = (f32[4,24,4]{2,1,0:T(8,128)S(1)}, f32[4,24,4]{2,1,0:T(8,128)S(1)}, u32[]{:S(2)}, u32[]{:S(2)}) collective-permute-start(f32[4,24,4]{2,1,0:T(8,128)S(1)} %get-tuple-element.34), channel_id=1, source_target_pairs={{0,1},{1,2},{2,3},{3,4},{4,5},{5,6},{6,7},{8,9},{9,10},{10,11},{11... | collective-permute-start | bytes 4616 | tf_op jit(solution)/shard_map/ppermute | solution.py:22
  111.9 2.0 collective-permute-done.6
  116.6 5.4 %slice.461 = f32[4,16,516]{2,0,1:T(4,128)S(1)} slice(f32[4,16,1032]{2,0,1:T(4,128)S(1)} %bitcast.60), slice={[0:4:1], [0:16:1], [0:1032:2]} | slice | bytes 264192 | tf_op jit(solution)/shard_map/slice | solution.py:37
  122.0 5.5 %slice.463 = f32[4,16,516]{2,0,1:T(4,128)S(1)} slice(f32[4,16,1032]{2,0,1:T(4,128)S(1)} %bitcast.61), slice={[0:4:1], [0:16:1], [1:1032:2]} | slice | bytes 264192 | tf_op jit(solution)/shard_map/slice | solution.py:38
  128.4 2.3 copy.62
  130.7 7.7 %slice.475 = f32[4,8,512]{1,2,0:T(8,128)S(1)} slice(f32[4,16,1024]{1,2,0:T(8,128)} %bitcast.57), slice={[0:4:1], [0:16:2], [0:1024:2]} | slice | bytes 131072 | tf_op jit(solution)/shard_map/slice | solution.py:84
  144.2 5.5 %collective-permute-start.8 = (f32[4,4,512]{2,1,0:T(4,128)S(1)}, f32[4,4,512]{2,1,0:T(4,128)S(1)}, u32[]{:S(2)}, u32[]{:S(2)}) collective-permute-start(f32[4,4,512]{2,1,0:T(4,128)S(1)} %copy.63), channel_id=1, source_target_pairs={{0,8},{8,16},{16,24},{1,9},{9,17},{17,25},{2,10},{10,18},{18,26},{... | collective-permute-start | bytes 98312 | tf_op jit(solution)/shard_map/ppermute | solution.py:22
  150.9 2.7 collective-permute-start.10
  153.6 3.7 %collective-permute-start.11 = (f32[4,16,4]{2,1,0:T(8,128)S(1)}, f32[4,16,4]{2,1,0:T(8,128)S(1)}, u32[]{:S(2)}, u32[]{:S(2)}) collective-permute-start(f32[4,16,4]{2,1,0:T(8,128)S(1)} %get-tuple-element.48), channel_id=1, source_target_pairs={{1,0},{2,1},{3,2},{4,3},{5,4},{6,5},{7,6},{9,8},{10,9},{11,10},{12... | collective-permute-start | bytes 3080 | tf_op jit(solution)/shard_map/ppermute | solution.py:25
  157.3 31.5 %copy.55 = f32[4,32,1024,2]{0,3,2,1:T(2,128)} copy(f32[4,32,1024,2]{2,0,1,3:T(4,128)S(1)} %pad_maximum_fusion.3) | data formatting | bytes 2097152 | tf_op jit(solution)/shard_map/stack | solution.py:53
  188.9 8.5 %copy.61 = f32[4,16,512,2]{0,3,2,1:T(2,128)} copy(f32[4,16,512,2]{2,0,1,3:T(4,128)S(1)} %pad_maximum_fusion.7) | data formatting | bytes 524288 | tf_op jit(solution)/shard_map/stack | solution.py:53
  202.4 3.1 %copy.71 = f32[8,512,4]{2,1,0:T(8,128)S(1)} copy(f32[8,512,4]{0,1,2:T(8,128)S(1)} %bitcast.58) | data formatting | bytes 131072 | tf_op jit(solution)/shard_map/reshape | solution.py:56
  205.5 17.2 %scatter_fusion = f32[4,16384]{0,1:T(8,128)} fusion(f32[4,16384]{0,1:T(8,128)} %bitcast.53, s32[4096]{0:T(1024)S(1)} %bitcast.64, f32[4096,4]{1,0:T(8,128)S(1)} %bitcast.59), kind=kCustom, calls=%fused_computation | custom fusion | bytes 212992
  222.7 62.8 %scatter_custom_fusion.1 = f32[4,65536]{0,1:T(8,128)} fusion(f32[4,65536]{0,1:T(8,128)} %bitcast.51, s32[16384]{0:T(1024)S(1)} %bitcast.65, f32[4,16384]{0,1:T(8,128)} %scatter_fusion), kind=kCustom, calls=%fused_computation.2 | custom fusion | bytes 9437184
  285.4 20.3 %copy.70 = f32[4,32,2048]{2,1,0:T(8,128)} copy(f32[4,32,2048]{0,2,1:T(8,128)} %bitcast.52) | data formatting | bytes 2097152 | tf_op jit(solution)/shard_map/scatter | solution.py:87
  (129 shorter events, 33.3 us)
Async XLA Ops:
  0.0 11.2 %copy-start.1 = (f32[4,32,2048]{2,1,0:T(8,128)S(1)}, f32[4,32,2048]{2,1,0:T(8,128)}, u32[]{:S(2)}) copy-start(f32[4,32,2048]{2,1,0:T(8,128)} %param.1) | copy-start | bytes 3145732
  1.2 7.9 %collective-permute-start = (f32[4,4,2048]{2,1,0:T(4,128)S(1)}, f32[4,4,2048]{2,1,0:T(4,128)S(1)}, u32[]{:S(2)}, u32[]{:S(2)}) collective-permute-start(f32[4,4,2048]{2,1,0:T(4,128)S(1)} %get-tuple-element.19), channel_id=1, source_target_pairs={{0,8},{8,16},{16,24},{1,9},{9,17},{17,25},{2,10},{10,18},{18,26},{... | collective-permute-start | bytes 393224 | tf_op jit(solution)/shard_map/ppermute | solution.py:22
  4.9 6.3 %collective-permute-start.1 = (f32[4,4,2048]{2,1,0:T(4,128)S(1)}, f32[4,4,2048]{2,1,0:T(4,128)S(1)}, u32[]{:S(2)}, u32[]{:S(2)}) collective-permute-start(f32[4,4,2048]{2,1,0:T(4,128)S(1)} %get-tuple-element.20), channel_id=1, source_target_pairs={{8,0},{16,8},{24,16},{9,1},{17,9},{25,17},{10,2},{18,10},{26,18},{... | collective-permute-start | bytes 393224 | tf_op jit(solution)/shard_map/ppermute | solution.py:25
  11.4 1.1 copy-start
  12.5 5.9 %collective-permute-start.3 = (f32[4,40,4]{2,1,0:T(8,128)S(1)}, f32[4,40,4]{2,1,0:T(8,128)S(1)}, u32[]{:S(2)}, u32[]{:S(2)}) collective-permute-start(f32[4,40,4]{2,1,0:T(8,128)S(1)} %get-tuple-element.15), channel_id=1, source_target_pairs={{1,0},{2,1},{3,2},{4,3},{5,4},{6,5},{7,6},{9,8},{10,9},{11,10},{12... | collective-permute-start | bytes 7688 | tf_op jit(solution)/shard_map/ppermute | solution.py:25
  15.5 6.1 %collective-permute-start.2 = (f32[4,40,4]{2,1,0:T(8,128)S(1)}, f32[4,40,4]{2,1,0:T(8,128)S(1)}, u32[]{:S(2)}, u32[]{:S(2)}) collective-permute-start(f32[4,40,4]{2,1,0:T(8,128)S(1)} %get-tuple-element.16), channel_id=1, source_target_pairs={{0,1},{1,2},{2,3},{3,4},{4,5},{5,6},{6,7},{8,9},{9,10},{10,11},{11... | collective-permute-start | bytes 7688 | tf_op jit(solution)/shard_map/ppermute | solution.py:22
  98.4 6.2 %collective-permute-start.5 = (f32[4,4,1024]{2,1,0:T(4,128)}, f32[4,4,1024]{2,1,0:T(4,128)S(1)}, u32[]{:S(2)}, u32[]{:S(2)}) collective-permute-start(f32[4,4,1024]{2,1,0:T(4,128)} %copy.58), channel_id=1, source_target_pairs={{8,0},{16,8},{24,16},{9,1},{17,9},{25,17},{10,2},{18,10},{26,18},{... | collective-permute-start | bytes 196616 | tf_op jit(solution)/shard_map/ppermute | solution.py:25
  100.3 5.0 %collective-permute-start.4 = (f32[4,4,1024]{2,1,0:T(4,128)S(1)}, f32[4,4,1024]{2,1,0:T(4,128)}, u32[]{:S(2)}, u32[]{:S(2)}) collective-permute-start(f32[4,4,1024]{2,1,0:T(4,128)S(1)} %copy.57), channel_id=1, source_target_pairs={{0,8},{8,16},{16,24},{1,9},{9,17},{17,25},{2,10},{10,18},{18,26},{... | collective-permute-start | bytes 196616 | tf_op jit(solution)/shard_map/ppermute | solution.py:22
  104.0 7.8 %copy-start.3 = (s32[512]{0:T(512)S(1)}, s32[512]{0:T(512)}, u32[]{:S(2)}) copy-start(s32[512]{0:T(512)} %iota_multiply_fusion.1) | copy-start | bytes 6148
  104.0 7.8 %copy-start.5 = (s32[2]{0:T(128)S(1)}, s32[2]{0:T(128)}, u32[]{:S(2)}) copy-start(s32[2]{0:T(128)} %constant.6) | copy-start | bytes 28
  106.3 5.6 %collective-permute-start.7 = (f32[4,24,4]{2,1,0:T(8,128)S(1)}, f32[4,24,4]{2,1,0:T(8,128)S(1)}, u32[]{:S(2)}, u32[]{:S(2)}) collective-permute-start(f32[4,24,4]{2,1,0:T(8,128)S(1)} %get-tuple-element.33), channel_id=1, source_target_pairs={{1,0},{2,1},{3,2},{4,3},{5,4},{6,5},{7,6},{9,8},{10,9},{11,10},{12... | collective-permute-start | bytes 4616 | tf_op jit(solution)/shard_map/ppermute | solution.py:25
  108.2 5.7 %collective-permute-start.6 = (f32[4,24,4]{2,1,0:T(8,128)S(1)}, f32[4,24,4]{2,1,0:T(8,128)S(1)}, u32[]{:S(2)}, u32[]{:S(2)}) collective-permute-start(f32[4,24,4]{2,1,0:T(8,128)S(1)} %get-tuple-element.34), channel_id=1, source_target_pairs={{0,1},{1,2},{2,3},{3,4},{4,5},{5,6},{6,7},{8,9},{9,10},{10,11},{11... | collective-permute-start | bytes 4616 | tf_op jit(solution)/shard_map/ppermute | solution.py:22
  139.8 10.0 %copy-start.4 = (s32[2]{0:T(128)S(1)}, s32[2]{0:T(128)}, u32[]{:S(2)}) copy-start(s32[2]{0:T(128)} %constant.3) | copy-start | bytes 28
  141.4 15.9 %copy-start.2 = (s32[2,8,8,128]{3,2,1,0:T(8,128)S(1)}, s32[2,8,8,128]{3,2,1,0:T(8,128)}, u32[]{:S(2)}) copy-start(s32[2,8,8,128]{3,2,1,0:T(8,128)} %select_bitcast_fusion) | copy-start | bytes 196612
  142.3 7.8 %collective-permute-start.9 = (f32[4,4,512]{2,1,0:T(4,128)}, f32[4,4,512]{2,1,0:T(4,128)S(1)}, u32[]{:S(2)}, u32[]{:S(2)}) collective-permute-start(f32[4,4,512]{2,1,0:T(4,128)} %copy.64), channel_id=1, source_target_pairs={{8,0},{16,8},{24,16},{9,1},{17,9},{25,17},{10,2},{18,10},{26,18},{... | collective-permute-start | bytes 98312 | tf_op jit(solution)/shard_map/ppermute | solution.py:25
  144.2 6.5 %collective-permute-start.8 = (f32[4,4,512]{2,1,0:T(4,128)S(1)}, f32[4,4,512]{2,1,0:T(4,128)S(1)}, u32[]{:S(2)}, u32[]{:S(2)}) collective-permute-start(f32[4,4,512]{2,1,0:T(4,128)S(1)} %copy.63), channel_id=1, source_target_pairs={{0,8},{8,16},{16,24},{1,9},{9,17},{17,25},{2,10},{10,18},{18,26},{... | collective-permute-start | bytes 98312 | tf_op jit(solution)/shard_map/ppermute | solution.py:22
  150.9 46.6 %collective-permute-start.10 = (f32[4,16,4]{2,1,0:T(8,128)S(1)}, f32[4,16,4]{2,1,0:T(8,128)S(1)}, u32[]{:S(2)}, u32[]{:S(2)}) collective-permute-start(f32[4,16,4]{2,1,0:T(8,128)S(1)} %get-tuple-element.47), channel_id=1, source_target_pairs={{0,1},{1,2},{2,3},{3,4},{4,5},{5,6},{6,7},{8,9},{9,10},{10,11},{11... | collective-permute-start | bytes 3080 | tf_op jit(solution)/shard_map/ppermute | solution.py:22
  153.6 43.8 %collective-permute-start.11 = (f32[4,16,4]{2,1,0:T(8,128)S(1)}, f32[4,16,4]{2,1,0:T(8,128)S(1)}, u32[]{:S(2)}, u32[]{:S(2)}) collective-permute-start(f32[4,16,4]{2,1,0:T(8,128)S(1)} %get-tuple-element.48), channel_id=1, source_target_pairs={{1,0},{2,1},{3,2},{4,3},{5,4},{6,5},{7,6},{9,8},{10,9},{11,10},{12... | collective-permute-start | bytes 3080 | tf_op jit(solution)/shard_map/ppermute | solution.py:25
where the time goes:
time: 308 us; the launch traced here: 306 us
  local copies, waits for them, and re-layouts  250 us (81%)
  starting transfers between devices  35.8 us (12%)
  other arithmetic  10.5 us (3%)
  waiting for transfers between devices  8.65 us (3%)
    unnamed x16, local copies, waits for them, and re-layouts  81.1 us
    another operation x8, local copies, waits for them, and re-layouts, lifting(): paired = jnp.stack([lowpass, highpass], axis=along + 1)  48 us
    slice x6, local copies, waits for them, and re-layouts, lifting(): odds = lax.slice_in_dim(extended, 1, length, 2, along)  25.7 us
    slice x6, local copies, waits for them, and re-layouts, lifting(): evens = lax.slice_in_dim(extended, 0, length, 2, along)  25.6 us
    slice x4, local copies, waits for them, and re-layouts, shards(): lowband = transformed[:, ::2, ::2]  24.2 us
    ppermute x6, starting transfers between devices, with_halo(): lax.ppermute(lax.slice_in_dim(block, block.shape[dim] - width, None, axis...  21.4 us
    scatter x1, local copies, waits for them, and re-layouts, shards(): combined = transformed.at[:, ::2, ::2].set(combined)  20.3 us
    ppermute x6, starting transfers between devices, with_halo(): lax.ppermute(lax.slice_in_dim(block, 0, width, axis=dim), axis, backward)  14.3 us
  transfers between devices with their start and end apart: 12, of which 5 were waited for; matrix products, arithmetic and copies ran while one was open for 14% of the time, Pallas kernels for 0%

commit v1 on v0

v1 whole, which is shorter than its diff:
```python
import functools

import jax
import jax.numpy as jnp
from jax import lax
from jax.experimental import pallas as pl
from jax.experimental.pallas import tpu as pltpu
from jax.sharding import PartitionSpec as P

LEVELS = 3
PREDICT_ONE = -1.586134342
UPDATE_ONE = -0.05298011854
PREDICT_TWO = 0.8829110762
UPDATE_TWO = 0.4435068522
SCALE_HIGH = 1.230174105
SCALE_LOW = 1.0 / 1.230174105
STEPS = (PREDICT_ONE, UPDATE_ONE, PREDICT_TWO, UPDATE_TWO)

SUB, LANE = 8, 128
ABOVE, BELOW = 28, 21


def row_cascade(rows, own, at_top, at_bottom):
    levels = []
    for level in range(LEVELS):
        dist = 1 << level
        for step, factor in enumerate(STEPS):
            first = dist if step % 2 == 0 else 0
            for r in sorted(rows):
                if (r - first) % (2 * dist) or r - dist not in rows or r + dist not in rows:
                    continue
                before, after = rows[r - dist], rows[r + dist]
                if r == 0:
                    before = jnp.where(at_top, after, before)
                if r == own - dist:
                    after = jnp.where(at_bottom, before, after)
                rows[r] = rows[r] + factor * (before + after)
            if step:
                edge = min(rows), max(rows)
                rows = {r: v for r, v in rows.items() if edge[0] < r < edge[1]}
        lows = {r: v * SCALE_LOW for r, v in rows.items() if r % (2 * dist) == 0}
        levels.append({
            r: lows[r] if r % (2 * dist) == 0 else rows[r] * SCALE_HIGH
            for r in range(0, own, dist)
        })
        rows = lows
    return levels


def lane_level(tiles, level, masks):
    dist = 1 << level
    lane, at_left, at_right = masks
    count = len(tiles)
    odd = (lane // dist) % 2 == 1
    low_edge, high_edge = lane < dist, lane >= LANE - dist
    for step, factor in enumerate(STEPS):
        weight = jnp.where(odd if step % 2 == 0 else ~odd, factor, 0.0)
        fwd = [pltpu.roll(t, dist, 1) for t in tiles]
        bwd = [pltpu.roll(t, LANE - dist, 1) for t in tiles]
        fresh = []
        for q in range(count):
            left = jnp.where(low_edge, fwd[q - 1], fwd[q])
            right = jnp.where(high_edge, bwd[(q + 1) % count], bwd[q])
            if q == 1:
                left = jnp.where(at_left & low_edge, right, left)
            if q == count - 1:
                right = jnp.where(at_right & high_edge, left, right)
            fresh.append(tiles[q] + weight * (left + right))
        tiles = fresh
    scale = jnp.where(odd, SCALE_HIGH, SCALE_LOW)
    return [t * scale for t in tiles]


def kernel(nr, nc, x, out, held, done, *rest):
    banks, (send_sem, recv_sem, out_sem) = rest[:LEVELS], rest[LEVELS:]
    images, bands, tiles = x.shape[0], x.shape[1], x.shape[2]
    half = tiles // 2
    width = half + 2
    own = bands * SUB
    below = -(-BELOW // SUB)
    r_at, c_at = lax.axis_index("row"), lax.axis_index("col")

    def inside(dr, dc):
        ok = []
        if dr:
            ok.append(r_at > 0 if dr < 0 else r_at < nr - 1)
        if dc:
            ok.append(c_at > 0 if dc < 0 else c_at < nc - 1)
        return ok[0] if len(ok) == 1 else ok[0] & ok[1]

    around = [(dr, dc) for dr in (-1, 0, 1) for dc in (-1, 0, 1) if dr or dc]
    barrier = pltpu.get_barrier_semaphore()
    total = jnp.int32(0)
    for dr, dc in around:
        ok = inside(dr, dc)
        total = total + ok.astype(jnp.int32)

        @pl.when(ok)
        def _():
            pl.semaphore_signal(
                barrier, inc=1, device_id=(r_at + dr, c_at + dc),
                device_id_type=pl.DeviceIdType.MESH,
            )

    row_part = {
        -1: (pl.ds(0, bands), pl.ds(0, bands)),
        0: (pl.ds(0, bands), pl.ds(bands, bands)),
        1: (pl.ds(0, below), pl.ds(2 * bands, below)),
    }
    col_part = (
        (0, 0, pl.ds(0, half + 1), pl.ds(1, half + 1)),
        (0, 1, pl.ds(half - 1, half + 1), pl.ds(0, half + 1)),
        (-1, 0, pl.ds(tiles - 1, 1), pl.ds(0, 1)),
        (1, 1, pl.ds(0, 1), pl.ds(width - 1, 1)),
    )
    parts = [
        (dr, dc, x.at[:, src_r, src_c], held.at[h, :, dst_r, dst_c])
        for dr, (src_r, dst_r) in row_part.items()
        for dc, h, src_c, dst_c in col_part
    ]

    def local(n):
        return pltpu.make_async_copy(parts[n][2], parts[n][3], recv_sem.at[n])

    def remote(n):
        dr, dc, src, dst = parts[n]
        return pltpu.make_async_remote_copy(
            src_ref=src, dst_ref=dst, send_sem=send_sem.at[n], recv_sem=recv_sem.at[n],
            device_id=(r_at - dr, c_at - dc), device_id_type=pl.DeviceIdType.MESH,
        )

    for n, (dr, dc, _, _) in enumerate(parts):
        if not (dr or dc):
            local(n).start()
    pl.semaphore_wait(barrier, total)
    for n, (dr, dc, _, _) in enumerate(parts):
        if dr or dc:
            @pl.when(inside(-dr, -dc))
            def _():
                remote(n).start()
    for n, (dr, dc, _, _) in enumerate(parts):
        if dr or dc:
            @pl.when(inside(dr, dc))
            def _():
                remote(n).wait_recv()
        else:
            local(n).wait()

    strands = 2 * images
    pitch = (2 * bands + below) * width * SUB
    flat = held.reshape(strands * pitch, LANE)
    lane = lax.broadcasted_iota(jnp.int32, (strands, LANE), 1)
    strand = lax.broadcasted_iota(jnp.int32, (strands, LANE), 0)
    at_top = jnp.broadcast_to(r_at == 0, (strands, LANE))
    at_bottom = jnp.broadcast_to(r_at == nr - 1, (strands, LANE))
    at_left = (strand < images) & (c_at == 0)
    at_right = (strand >= images) & (c_at == nc - 1)

    def fetch(r, t):
        at = r + own
        start = ((at // SUB) * width + t) * SUB + at % SUB
        return flat[pl.ds(start, strands, stride=pitch), :]

    span = range(-ABOVE, own + BELOW)

    def keep(rows, q):
        for level, found in enumerate(row_cascade(rows, own, at_top, at_bottom)):
            for r, value in found.items():
                banks[level][r >> level, q] = value

    keep({r: jnp.where(lane < LANE // 2, fetch(r, width - 1), fetch(r, 0)) for r in span}, 0)

    def columns(q, carry):
        keep({r: fetch(r, q) for r in span}, q)
        return carry

    lax.fori_loop(1, half + 1, columns, 0)

    masks = (lane, at_left, at_right)
    stretch = bands * half * SUB
    target = done.reshape(strands * stretch, LANE)
    group = 1 << (LEVELS - 1)

    def bundle(i, carry):
        for k in range(group):
            r = i * group + k
            result = None
            for level in range(LEVELS):
                if k % (1 << level):
                    break
                row = i * (group >> level) + (k >> level)
                value = [banks[level][row, q] for q in range(half + 1)]
                for lower in range(level + 1):
                    value = lane_level(value, lower, masks)
                result = value if result is None else [
                    jnp.where(lane % (1 << level) == 0, new, old)
                    for new, old in zip(value, result)
                ]
            for q in range(half):
                start = ((r // SUB) * half + q) * SUB + r % SUB
                target[pl.ds(start, strands, stride=stretch), :] = result[q + 1]
        return carry

    lax.fori_loop(0, own // group, bundle, 0)

    copies = [
        pltpu.make_async_copy(done.at[h], out.at[:, :, pl.ds(h * half, half)], out_sem.at[h])
        for h in range(2)
    ]
    for copy in copies:
        copy.start()
    for n, (dr, dc, _, _) in enumerate(parts):
        if dr or dc:
            @pl.when(inside(-dr, -dc))
            def _():
                remote(n).wait_send()
    for copy in copies:
        copy.wait()


def shards(nr, nc, block):
    images, own, cols = block.shape
    bands, tiles = own // SUB, cols // LANE
    half = tiles // 2
    below = -(-BELOW // SUB)
    x = block.reshape(images, bands, SUB, tiles, LANE).transpose(0, 1, 3, 2, 4)
    y = pl.pallas_call(
        functools.partial(kernel, nr, nc),
        out_shape=jax.ShapeDtypeStruct(x.shape, x.dtype),
        in_specs=[pl.BlockSpec(memory_space=pl.ANY)],
        out_specs=pl.BlockSpec(memory_space=pl.ANY),
        scratch_shapes=[
            pltpu.VMEM((2, images, 2 * bands + below, half + 2, SUB, LANE), jnp.float32),
            pltpu.VMEM((2, images, bands, half, SUB, LANE), jnp.float32),
            *[pltpu.VMEM((own >> n, half + 1, 2 * images, LANE), jnp.float32) for n in range(LEVELS)],
            pltpu.SemaphoreType.DMA((12,)),
            pltpu.SemaphoreType.DMA((12,)),
            pltpu.SemaphoreType.DMA((2,)),
        ],
        compiler_params=pltpu.CompilerParams(collective_id=0, has_side_effects=True, vmem_limit_bytes=40 << 20),
    )(x)
    return y.transpose(0, 1, 3, 2, 4).reshape(images, own, cols)


def solution(mesh):
    return jax.shard_map(
        functools.partial(shards, mesh.shape["row"], mesh.shape["col"]),
        mesh=mesh,
        in_specs=(P(None, "row", "col"),),
        out_specs=P(None, "row", "col"),
        check_vma=False,
    )
```

time: 308 us -> 36 us (0.12)
  the two profiles are of different devices: /device:TPU:9 before, /device:TPU:6 now
where the time goes in v1:
time: 36 us; the launch traced here: 35.8 us
  Pallas kernels  33.6 us (93%)
  local copies, waits for them, and re-layouts  2.2 us (6%)
    pallas_call x1, Pallas kernels, shards(): pl.pallas_call(functools.partial(kernel, nr, nc), out_shape=jax.ShapeDtyp...  33.6 us
    unnamed x3, local copies, waits for them, and re-layouts  2.2 us

profile of v1, /device:TPU:6, one launch (start us, length us, event | category | flops | bytes accessed | tf_op | source)
XLA Modules:
  0.0 35.8 jit_solution(1854480458818817787)
XLA Ops:
  0.0 0.0 copy-start
  0.0 1.2 %copy-done = f32[4,32,2048]{2,1,0:T(8,128)S(1)} copy-done((f32[4,32,2048]{2,1,0:T(8,128)S(1)}, f32[4,32,2048]{2,1,0:T(8,128)}, u32[]{:S(2)}) %copy-start) | copy-done | bytes 1048600
  1.2 33.6 %shard_map.17 = f32[4,4,16,8,128]{4,3,2,1,0:T(8,128)S(1)} custom-call(f32[4,4,16,8,128]{4,3,2,1,0:T(8,128)S(1)} %bitcast.7), custom_call_target="tpu_custom_call" | custom-call | tf_op jit(solution)/shard_map/pallas_call | solution.py:227
  34.9 1.0 %copy.3 = f32[4,32,2048]{2,1,0:T(8,128)} copy(f32[4,32,2048]{2,1,0:T(8,128)S(1)} %bitcast.6) | data formatting | bytes 2097152
Async XLA Ops:
  0.0 1.2 %copy-start = (f32[4,32,2048]{2,1,0:T(8,128)S(1)}, f32[4,32,2048]{2,1,0:T(8,128)}, u32[]{:S(2)}) copy-start(f32[4,32,2048]{2,1,0:T(8,128)} %param.1) | copy-start | bytes 3145732

commit v2 on v1

--- a/solution.py
+++ b/solution.py
@@ -17,34 +17,20 @@
 STEPS = (PREDICT_ONE, UPDATE_ONE, PREDICT_TWO, UPDATE_TWO)
 
 SUB, LANE = 8, 128
-ABOVE, BELOW = 28, 21
-
-
-def row_cascade(rows, own, at_top, at_bottom):
-    levels = []
-    for level in range(LEVELS):
-        dist = 1 << level
-        for step, factor in enumerate(STEPS):
-            first = dist if step % 2 == 0 else 0
-            for r in sorted(rows):
-                if (r - first) % (2 * dist) or r - dist not in rows or r + dist not in rows:
-                    continue
-                before, after = rows[r - dist], rows[r + dist]
-                if r == 0:
-                    before = jnp.where(at_top, after, before)
-                if r == own - dist:
-                    after = jnp.where(at_bottom, before, after)
-                rows[r] = rows[r] + factor * (before + after)
-            if step:
-                edge = min(rows), max(rows)
-                rows = {r: v for r, v in rows.items() if edge[0] < r < edge[1]}
-        lows = {r: v * SCALE_LOW for r, v in rows.items() if r % (2 * dist) == 0}
-        levels.append({
-            r: lows[r] if r % (2 * dist) == 0 else rows[r] * SCALE_HIGH
-            for r in range(0, own, dist)
-        })
-        rows = lows
-    return levels
+REACH = 4
+
+
+def row_level(rows, count, at_top, at_bottom):
+    rows = dict(rows)
+    for step, factor in enumerate(STEPS):
+        for r in range(-REACH + 1 + step, count + REACH - 2 - step, 2):
+            before, after = rows[r - 1], rows[r + 1]
+            if r == 0:
+                before = jnp.where(at_top, after, before)
+            if r == count - 1:
+                after = jnp.where(at_bottom, before, after)
+            rows[r] = rows[r] + factor * (before + after)
+    return [rows[r] * (SCALE_HIGH if r % 2 else SCALE_LOW) for r in range(count)]
 
 
 def lane_level(tiles, level, masks):
@@ -72,12 +58,12 @@
 
 
 def kernel(nr, nc, x, out, held, done, *rest):
-    banks, (send_sem, recv_sem, out_sem) = rest[:LEVELS], rest[LEVELS:]
+    banks, rest = rest[:LEVELS], rest[LEVELS:]
+    edges, (send_sem, recv_sem, out_sem) = rest[:-3], rest[-3:]
     images, bands, tiles = x.shape[0], x.shape[1], x.shape[2]
     half = tiles // 2
     width = half + 2
     own = bands * SUB
-    below = -(-BELOW // SUB)
     r_at, c_at = lax.axis_index("row"), lax.axis_index("col")
 
     def inside(dr, dc):
@@ -103,9 +89,9 @@
             )
 
     row_part = {
-        -1: (pl.ds(0, bands), pl.ds(0, bands)),
-        0: (pl.ds(0, bands), pl.ds(bands, bands)),
-        1: (pl.ds(0, below), pl.ds(2 * bands, below)),
+        -1: (pl.ds(bands - 1, 1), pl.ds(0, 1)),
+        0: (pl.ds(0, bands), pl.ds(1, bands)),
+        1: (pl.ds(0, 1), pl.ds(bands + 1, 1)),
     }
     col_part = (
         (0, 0, pl.ds(0, half + 1), pl.ds(1, half + 1)),
@@ -147,7 +133,7 @@
             local(n).wait()
 
     strands = 2 * images
-    pitch = (2 * bands + below) * width * SUB
+    pitch = (bands + 2) * width * SUB
     flat = held.reshape(strands * pitch, LANE)
     lane = lax.broadcasted_iota(jnp.int32, (strands, LANE), 1)
     strand = lax.broadcasted_iota(jnp.int32, (strands, LANE), 0)
@@ -155,53 +141,93 @@
     at_bottom = jnp.broadcast_to(r_at == nr - 1, (strands, LANE))
     at_left = (strand < images) & (c_at == 0)
     at_right = (strand >= images) & (c_at == nc - 1)
-
-    def fetch(r, t):
-        at = r + own
-        start = ((at // SUB) * width + t) * SUB + at % SUB
-        return flat[pl.ds(start, strands, stride=pitch), :]
-
-    span = range(-ABOVE, own + BELOW)
-
-    def keep(rows, q):
-        for level, found in enumerate(row_cascade(rows, own, at_top, at_bottom)):
-            for r, value in found.items():
-                banks[level][r >> level, q] = value
-
-    keep({r: jnp.where(lane < LANE // 2, fetch(r, width - 1), fetch(r, 0)) for r in span}, 0)
-
-    def columns(q, carry):
-        keep({r: fetch(r, q) for r in span}, q)
-        return carry
-
-    lax.fori_loop(1, half + 1, columns, 0)
-
     masks = (lane, at_left, at_right)
     stretch = bands * half * SUB
     target = done.reshape(strands * stretch, LANE)
-    group = 1 << (LEVELS - 1)
-
-    def bundle(i, carry):
-        for k in range(group):
-            r = i * group + k
-            result = None
-            for level in range(LEVELS):
-                if k % (1 << level):
-                    break
-                row = i * (group >> level) + (k >> level)
+
+    def fetch(r, t):
+        at = r + SUB
+        start = ((at // SUB) * width + t) * SUB + at % SUB
+        return flat[pl.ds(start, strands, stride=pitch), :]
+
+    def keep(level, rows, q):
+        count = own >> level
+        found = row_level(rows, count, at_top, at_bottom)
+        for r, value in enumerate(found):
+            banks[level][r, q] = value
+        if level < LEVELS - 1:
+            lows = found[::2]
+            up, down = edges[4 * level], edges[4 * level + 1]
+            for r in range(REACH - 1):
+                up[r, q] = lows[r]
+            for r in range(REACH):
+                down[r, q] = lows[len(lows) - REACH + r]
+
+    def passing(level, n):
+        at = 12 + 2 * level + n
+        return pltpu.make_async_remote_copy(
+            src_ref=edges[4 * level + n], dst_ref=edges[4 * level + 2 + n],
+            send_sem=send_sem.at[at], recv_sem=recv_sem.at[at],
+            device_id=(r_at - 1 + 2 * n, c_at), device_id_type=pl.DeviceIdType.MESH,
+        )
+
+    def send(level):
+        for n in range(2):
+            @pl.when(inside(2 * n - 1, 0))
+            def _():
+                passing(level, n).start()
+
+    def receive(level):
+        for n in range(2):
+            @pl.when(inside(1 - 2 * n, 0))
+            def _():
+                passing(level, n).wait_recv()
+
+    span = range(-REACH, own + REACH - 1)
+    keep(0, {r: jnp.where(lane < LANE // 2, fetch(r, width - 1), fetch(r, 0)) for r in span}, 0)
+
+    def first_rows(q, carry):
+        keep(0, {r: fetch(r, q) for r in span}, q)
+        return carry
+
+    lax.fori_loop(1, half + 1, first_rows, 0)
+
+    for level in range(LEVELS):
+        dist = 1 << level
+        if level < LEVELS - 1:
+            send(level)
+
+        def lanes(i, carry):
+            for k in range(2):
+                row = 2 * i + k
                 value = [banks[level][row, q] for q in range(half + 1)]
                 for lower in range(level + 1):
                     value = lane_level(value, lower, masks)
-                result = value if result is None else [
-                    jnp.where(lane % (1 << level) == 0, new, old)
-                    for new, old in zip(value, result)
-                ]
-            for q in range(half):
-                start = ((r // SUB) * half + q) * SUB + r % SUB
-                target[pl.ds(start, strands, stride=stretch), :] = result[q + 1]
-        return carry
-
-    lax.fori_loop(0, own // group, bundle, 0)
+                r = row * dist
+                for q in range(half):
+                    start = ((r // SUB) * half + q) * SUB + r % SUB
+                    at = pl.ds(start, strands, stride=stretch)
+                    new = value[q + 1]
+                    if level:
+                        new = jnp.where(lane % dist == 0, new, target[at, :])
+                    target[at, :] = new
+            return carry
+
+        lax.fori_loop(0, (own >> level) // 2, lanes, 0)
+        if level < LEVELS - 1:
+            receive(level)
+            count = own >> (level + 1)
+
+            def next_rows(q, carry):
+                rows = {r: banks[level][2 * r, q] for r in range(count)}
+                for r in range(REACH):
+                    rows[r - REACH] = edges[4 * level + 3][r, q]
+                for r in range(REACH - 1):
+                    rows[count + r] = edges[4 * level + 2][r, q]
+                keep(level + 1, rows, q)
+                return carry
+
+            lax.fori_loop(0, half + 1, next_rows, 0)
 
     copies = [
         pltpu.make_async_copy(done.at[h], out.at[:, :, pl.ds(h * half, half)], out_sem.at[h])
@@ -214,6 +240,11 @@
             @pl.when(inside(-dr, -dc))
             def _():
                 remote(n).wait_send()
+    for level in range(LEVELS - 1):
+        for n in range(2):
+            @pl.when(inside(2 * n - 1, 0))
+            def _():
+                passing(level, n).wait_send()
     for copy in copies:
         copy.wait()
 
@@ -222,7 +253,6 @@
     images, own, cols = block.shape
     bands, tiles = own // SUB, cols // LANE
     half = tiles // 2
-    below = -(-BELOW // SUB)
     x = block.reshape(images, bands, SUB, tiles, LANE).transpose(0, 1, 3, 2, 4)
     y = pl.pallas_call(
         functools.partial(kernel, nr, nc),
@@ -230,11 +260,15 @@
         in_specs=[pl.BlockSpec(memory_space=pl.ANY)],
         out_specs=pl.BlockSpec(memory_space=pl.ANY),
         scratch_shapes=[
-            pltpu.VMEM((2, images, 2 * bands + below, half + 2, SUB, LANE), jnp.float32),
+            pltpu.VMEM((2, images, bands + 2, half + 2, SUB, LANE), jnp.float32),
             pltpu.VMEM((2, images, bands, half, SUB, LANE), jnp.float32),
             *[pltpu.VMEM((own >> n, half + 1, 2 * images, LANE), jnp.float32) for n in range(LEVELS)],
-            pltpu.SemaphoreType.DMA((12,)),
-            pltpu.SemaphoreType.DMA((12,)),
+            *[
+                pltpu.VMEM((n, half + 1, 2 * images, LANE), jnp.float32)
+                for n in (REACH - 1, REACH) * (2 * (LEVELS - 1))
+            ],
+            pltpu.SemaphoreType.DMA((12 + 2 * (LEVELS - 1),)),
+            pltpu.SemaphoreType.DMA((12 + 2 * (LEVELS - 1),)),
             pltpu.SemaphoreType.DMA((2,)),
         ],
         compiler_params=pltpu.CompilerParams(collective_id=0, has_side_effects=True, vmem_limit_bytes=40 << 20),

time: 36 us -> 31.1 us (0.86)
  the two profiles are of different devices: /device:TPU:6 before, /device:TPU:9 now
where the time goes in v2:
time: 31.1 us; the launch traced here: 31 us
  Pallas kernels  28.8 us (93%)
  local copies, waits for them, and re-layouts  2.2 us (7%)
    pallas_call x1, Pallas kernels, shards(): pl.pallas_call(functools.partial(kernel, nr, nc), out_shape=jax.ShapeDtyp...  28.8 us
    unnamed x3, local copies, waits for them, and re-layouts  2.2 us

profile of v2, /device:TPU:9, one launch (start us, length us, event | category | flops | bytes accessed | tf_op | source)
XLA Modules:
  0.0 31.0 jit_solution(9301434151400964670)
XLA Ops:
  0.0 0.0 copy-start
  0.0 1.2 %copy-done = f32[4,32,2048]{2,1,0:T(8,128)S(1)} copy-done((f32[4,32,2048]{2,1,0:T(8,128)S(1)}, f32[4,32,2048]{2,1,0:T(8,128)}, u32[]{:S(2)}) %copy-start) | copy-done | bytes 1048600
  1.2 28.8 %shard_map.17 = f32[4,4,16,8,128]{4,3,2,1,0:T(8,128)S(1)} custom-call(f32[4,4,16,8,128]{4,3,2,1,0:T(8,128)S(1)} %bitcast.7), custom_call_target="tpu_custom_call" | custom-call | tf_op jit(solution)/shard_map/pallas_call | solution.py:257
  30.0 1.0 %copy.3 = f32[4,32,2048]{2,1,0:T(8,128)} copy(f32[4,32,2048]{2,1,0:T(8,128)S(1)} %bitcast.6) | data formatting | bytes 2097152
Async XLA Ops:
  0.0 1.2 %copy-start = (f32[4,32,2048]{2,1,0:T(8,128)S(1)}, f32[4,32,2048]{2,1,0:T(8,128)}, u32[]{:S(2)}) copy-start(f32[4,32,2048]{2,1,0:T(8,128)} %param.1) | copy-start | bytes 3145732

commit v3 on v2

--- a/solution.py
+++ b/solution.py
@@ -18,6 +18,8 @@
 
 SUB, LANE = 8, 128
 REACH = 4
+
+TRIPS = (8, 8, 8)
 
 
 def row_level(rows, count, at_top, at_bottom):
@@ -33,28 +35,32 @@
     return [rows[r] * (SCALE_HIGH if r % 2 else SCALE_LOW) for r in range(count)]
 
 
-def lane_level(tiles, level, masks):
+def lane_level(group, level, masks):
     dist = 1 << level
     lane, at_left, at_right = masks
-    count = len(tiles)
     odd = (lane // dist) % 2 == 1
     low_edge, high_edge = lane < dist, lane >= LANE - dist
+    mirror_left, mirror_right = at_left & low_edge, at_right & high_edge
     for step, factor in enumerate(STEPS):
         weight = jnp.where(odd if step % 2 == 0 else ~odd, factor, 0.0)
-        fwd = [pltpu.roll(t, dist, 1) for t in tiles]
-        bwd = [pltpu.roll(t, LANE - dist, 1) for t in tiles]
-        fresh = []
-        for q in range(count):
-            left = jnp.where(low_edge, fwd[q - 1], fwd[q])
-            right = jnp.where(high_edge, bwd[(q + 1) % count], bwd[q])
-            if q == 1:
-                left = jnp.where(at_left & low_edge, right, left)
-            if q == count - 1:
-                right = jnp.where(at_right & high_edge, left, right)
-            fresh.append(tiles[q] + weight * (left + right))
-        tiles = fresh
+        moved = []
+        for tiles in group:
+            count = len(tiles)
+            fwd = [pltpu.roll(t, dist, 1) for t in tiles]
+            bwd = [pltpu.roll(t, LANE - dist, 1) for t in tiles]
+            fresh = []
+            for q in range(count):
+                left = jnp.where(low_edge, fwd[q - 1], fwd[q])
+                right = jnp.where(high_edge, bwd[(q + 1) % count], bwd[q])
+                if q == 1:
+                    left = jnp.where(mirror_left, right, left)
+                if q == count - 1:
+                    right = jnp.where(mirror_right, left, right)
+                fresh.append(tiles[q] + weight * (left + right))
+            moved.append(fresh)
+        group = moved
     scale = jnp.where(odd, SCALE_HIGH, SCALE_LOW)
-    return [t * scale for t in tiles]
+    return [[t * scale for t in tiles] for tiles in group]
 
 
 def kernel(nr, nc, x, out, held, done, *rest):
@@ -194,26 +200,28 @@
 
     for level in range(LEVELS):
         dist = 1 << level
+        trip = TRIPS[level]
         if level < LEVELS - 1:
             send(level)
 
         def lanes(i, carry):
-            for k in range(2):
-                row = 2 * i + k
-                value = [banks[level][row, q] for q in range(half + 1)]
-                for lower in range(level + 1):
-                    value = lane_level(value, lower, masks)
-                r = row * dist
+            group = [
+                [banks[level][trip * i + k, q] for q in range(half + 1)] for k in range(trip)
+            ]
+            for lower in range(level + 1):
+                group = lane_level(group, lower, masks)
+            for k in range(trip):
+                r = (trip * i + k) * dist
                 for q in range(half):
                     start = ((r // SUB) * half + q) * SUB + r % SUB
                     at = pl.ds(start, strands, stride=stretch)
-                    new = value[q + 1]
+                    new = group[k][q + 1]
                     if level:
                         new = jnp.where(lane % dist == 0, new, target[at, :])
                     target[at, :] = new
             return carry
 
-        lax.fori_loop(0, (own >> level) // 2, lanes, 0)
+        lax.fori_loop(0, (own >> level) // trip, lanes, 0)
         if level < LEVELS - 1:
             receive(level)
             count = own >> (level + 1)

time: 31.1 us -> 22.2 us (0.71)
  Pallas kernels: 28.8 us -> 19.8 us
    pallas_call x1, Pallas kernels: 28.8 us -> 19.8 us  [shards(): pl.pallas_call(functools.partial(kernel, nr, nc), out_shape=jax.ShapeDtyp...]
where the time goes in v3:
time: 22.2 us; the launch traced here: 22 us
  Pallas kernels  19.8 us (89%)
  local copies, waits for them, and re-layouts  2.2 us (10%)
    pallas_call x1, Pallas kernels, shards(): pl.pallas_call(functools.partial(kernel, nr, nc), out_shape=jax.ShapeDtyp...  19.8 us
    unnamed x3, local copies, waits for them, and re-layouts  2.2 us

profile of v3, /device:TPU:9, one launch (start us, length us, event | category | flops | bytes accessed | tf_op | source)
XLA Modules:
  0.0 22.0 jit_solution(10757374255739388928)
XLA Ops:
  0.0 0.0 copy-start
  0.0 1.2 %copy-done = f32[4,32,2048]{2,1,0:T(8,128)S(1)} copy-done((f32[4,32,2048]{2,1,0:T(8,128)S(1)}, f32[4,32,2048]{2,1,0:T(8,128)}, u32[]{:S(2)}) %copy-start) | copy-done | bytes 1048600
  1.2 19.8 %shard_map.17 = f32[4,4,16,8,128]{4,3,2,1,0:T(8,128)S(1)} custom-call(f32[4,4,16,8,128]{4,3,2,1,0:T(8,128)S(1)} %bitcast.7), custom_call_target="tpu_custom_call" | custom-call | tf_op jit(solution)/shard_map/pallas_call | solution.py:265
  21.0 1.0 %copy.3 = f32[4,32,2048]{2,1,0:T(8,128)} copy(f32[4,32,2048]{2,1,0:T(8,128)S(1)} %bitcast.6) | data formatting | bytes 2097152
Async XLA Ops:
  0.0 1.2 %copy-start = (f32[4,32,2048]{2,1,0:T(8,128)S(1)}, f32[4,32,2048]{2,1,0:T(8,128)}, u32[]{:S(2)}) copy-start(f32[4,32,2048]{2,1,0:T(8,128)} %param.1) | copy-start | bytes 3145732

commit v4 on v3

--- a/solution.py
+++ b/solution.py
@@ -19,7 +19,7 @@
 SUB, LANE = 8, 128
 REACH = 4
 
-TRIPS = (8, 8, 8)
+TRIPS = (16, 16, 8)
 
 
 def row_level(rows, count, at_top, at_bottom):
@@ -35,32 +35,51 @@
     return [rows[r] * (SCALE_HIGH if r % 2 else SCALE_LOW) for r in range(count)]
 
 
-def lane_level(group, level, masks):
+def lane_levels(group, level, last, masks):
     dist = 1 << level
     lane, at_left, at_right = masks
-    odd = (lane // dist) % 2 == 1
-    low_edge, high_edge = lane < dist, lane >= LANE - dist
-    mirror_left, mirror_right = at_left & low_edge, at_right & high_edge
+    first = (lane & dist) == 0
+    head, tail = lane < 2 * dist, lane >= LANE - 2 * dist
+    mirror_left, mirror_right = at_left & head, at_right & tail
+    count = len(group[0])
+
+    def up(t, by):
+        return pltpu.roll(t, by, 1)
+
+    def down(t, by):
+        return pltpu.roll(t, LANE - by, 1)
+
+    pairs = list(zip(group[::2], group[1::2]))
+    even = [[jnp.where(first, x, up(y, dist)) for x, y in zip(*p)] for p in pairs]
+    odd = [[jnp.where(first, down(x, dist), y) for x, y in zip(*p)] for p in pairs]
     for step, factor in enumerate(STEPS):
-        weight = jnp.where(odd if step % 2 == 0 else ~odd, factor, 0.0)
-        moved = []
-        for tiles in group:
-            count = len(tiles)
-            fwd = [pltpu.roll(t, dist, 1) for t in tiles]
-            bwd = [pltpu.roll(t, LANE - dist, 1) for t in tiles]
-            fresh = []
-            for q in range(count):
-                left = jnp.where(low_edge, fwd[q - 1], fwd[q])
-                right = jnp.where(high_edge, bwd[(q + 1) % count], bwd[q])
-                if q == 1:
-                    left = jnp.where(mirror_left, right, left)
-                if q == count - 1:
-                    right = jnp.where(mirror_right, left, right)
-                fresh.append(tiles[q] + weight * (left + right))
-            moved.append(fresh)
-        group = moved
-    scale = jnp.where(odd, SCALE_HIGH, SCALE_LOW)
-    return [[t * scale for t in tiles] for tiles in group]
+        if step % 2 == 0:
+            for s, d in zip(even, odd):
+                far = [down(t, 2 * dist) for t in s]
+                for q in range(count):
+                    after = jnp.where(tail, far[(q + 1) % count], far[q])
+                    if q == count - 1:
+                        after = jnp.where(mirror_right, s[q], after)
+                    d[q] = d[q] + factor * (s[q] + after)
+        else:
+            for s, d in zip(even, odd):
+                far = [up(t, 2 * dist) for t in d]
+                for q in range(count):
+                    before = jnp.where(head, far[q - 1], far[q])
+                    if q == 1:
+                        before = jnp.where(mirror_left, d[q], before)
+                    s[q] = s[q] + factor * (before + d[q])
+    even = [[t * SCALE_LOW for t in s] for s in even]
+    result = []
+    if level < last:
+        for s in lane_levels(even, level + 1, last, masks):
+            result += [s, [down(t, dist) for t in s]]
+        return result
+    for s, d in zip(even, odd):
+        d = [t * SCALE_HIGH for t in d]
+        result.append([jnp.where(first, x, up(y, dist)) for x, y in zip(s, d)])
+        result.append([jnp.where(first, down(x, dist), y) for x, y in zip(s, d)])
+    return result
 
 
 def kernel(nr, nc, x, out, held, done, *rest):
@@ -95,9 +114,9 @@
             )
 
     row_part = {
-        -1: (pl.ds(bands - 1, 1), pl.ds(0, 1)),
-        0: (pl.ds(0, bands), pl.ds(1, bands)),
-        1: (pl.ds(0, 1), pl.ds(bands + 1, 1)),
+        -1: (pl.ds(bands - 1, 1), pl.ds(0, 1), pl.ds(SUB - REACH, REACH)),
+        0: (pl.ds(0, bands), pl.ds(1, bands), pl.ds(0, SUB)),
+        1: (pl.ds(0, 1), pl.ds(bands + 1, 1), pl.ds(0, REACH)),
     }
     col_part = (
         (0, 0, pl.ds(0, half + 1), pl.ds(1, half + 1)),
@@ -106,8 +125,8 @@
         (1, 1, pl.ds(0, 1), pl.ds(width - 1, 1)),
     )
     parts = [
-        (dr, dc, x.at[:, src_r, src_c], held.at[h, :, dst_r, dst_c])
-        for dr, (src_r, dst_r) in row_part.items()
+        (dr, dc, x.at[:, src_r, src_c, subs], held.at[h, :, dst_r, dst_c, subs])
+        for dr, (src_r, dst_r, subs) in row_part.items()
         for dc, h, src_c, dst_c in col_part
     ]
 
@@ -125,7 +144,9 @@
         if not (dr or dc):
             local(n).start()
     pl.semaphore_wait(barrier, total)
-    for n, (dr, dc, _, _) in enumerate(parts):
+    order = sorted(range(len(parts)), key=lambda n: parts[n][1] != 0)
+    for n in order:
+        dr, dc = parts[n][:2]
         if dr or dc:
             @pl.when(inside(-dr, -dc))
             def _():
@@ -208,8 +229,7 @@
             group = [
                 [banks[level][trip * i + k, q] for q in range(half + 1)] for k in range(trip)
             ]
-            for lower in range(level + 1):
-                group = lane_level(group, lower, masks)
+            group = lane_levels(group, 0, level, masks)
             for k in range(trip):
                 r = (trip * i + k) * dist
                 for q in range(half):
@@ -265,7 +285,7 @@
     y = pl.pallas_call(
         functools.partial(kernel, nr, nc),
         out_shape=jax.ShapeDtypeStruct(x.shape, x.dtype),
-        in_specs=[pl.BlockSpec(memory_space=pl.ANY)],
+        in_specs=[pl.BlockSpec(memory_space=pltpu.HBM)],
         out_specs=pl.BlockSpec(memory_space=pl.ANY),
         scratch_shapes=[
             pltpu.VMEM((2, images, bands + 2, half + 2, SUB, LANE), jnp.float32),

time: 22.2 us -> 21 us (0.946)
  Pallas kernels: 19.8 us -> 18.7 us
    pallas_call x1, Pallas kernels: 19.8 us -> 18.7 us  [shards(): pl.pallas_call(functools.partial(kernel, nr, nc), out_shape=jax.ShapeDtyp...]
where the time goes in v4:
time: 21 us; the launch traced here: 20.9 us
  Pallas kernels  18.7 us (89%)
  local copies, waits for them, and re-layouts  2.2 us (10%)
    pallas_call x1, Pallas kernels, shards(): pl.pallas_call(functools.partial(kernel, nr, nc), out_shape=jax.ShapeDtyp...  18.7 us
    unnamed x3, local copies, waits for them, and re-layouts  2.2 us

profile of v4, /device:TPU:9, one launch (start us, length us, event | category | flops | bytes accessed | tf_op | source)
XLA Modules:
  0.0 20.9 jit_solution(75739093293701123)
XLA Ops:
  0.0 0.0 copy-start
  0.0 1.2 %copy-done = f32[4,32,2048]{2,1,0:T(8,128)S(1)} copy-done((f32[4,32,2048]{2,1,0:T(8,128)S(1)}, f32[4,32,2048]{2,1,0:T(8,128)}, u32[]{:S(2)}) %copy-start) | copy-done | bytes 1048600
  1.2 18.7 %shard_map.17 = f32[4,4,16,8,128]{4,3,2,1,0:T(8,128)S(1)} custom-call(f32[4,4,16,8,128]{4,3,2,1,0:T(8,128)S(1)} %bitcast.7), custom_call_target="tpu_custom_call" | custom-call | tf_op jit(solution)/shard_map/pallas_call | solution.py:285
  19.9 1.0 %copy.3 = f32[4,32,2048]{2,1,0:T(8,128)} copy(f32[4,32,2048]{2,1,0:T(8,128)S(1)} %bitcast.6) | data formatting | bytes 2097152
Async XLA Ops:
  0.0 1.2 %copy-start = (f32[4,32,2048]{2,1,0:T(8,128)S(1)}, f32[4,32,2048]{2,1,0:T(8,128)}, u32[]{:S(2)}) copy-start(f32[4,32,2048]{2,1,0:T(8,128)} %param.1) | copy-start | bytes 3145732

commit v5 on v4

--- a/solution.py
+++ b/solution.py
@@ -190,25 +190,30 @@
             for r in range(REACH):
                 down[r, q] = lows[len(lows) - REACH + r]
 
-    def passing(level, n):
-        at = 12 + 2 * level + n
+    cut = half // 2 + 1
+    pieces = (pl.ds(0, cut), pl.ds(cut, half + 1 - cut))
+
+    def passing(level, n, piece):
+        at = 12 + 4 * level + 2 * n + piece
+        part = pieces[piece]
         return pltpu.make_async_remote_copy(
-            src_ref=edges[4 * level + n], dst_ref=edges[4 * level + 2 + n],
+            src_ref=edges[4 * level + n].at[:, part], dst_ref=edges[4 * level + 2 + n].at[:, part],
             send_sem=send_sem.at[at], recv_sem=recv_sem.at[at],
             device_id=(r_at - 1 + 2 * n, c_at), device_id_type=pl.DeviceIdType.MESH,
         )
 
-    def send(level):
+    def send(level, piece):
         for n in range(2):
             @pl.when(inside(2 * n - 1, 0))
             def _():
-                passing(level, n).start()
+                passing(level, n, piece).start()
 
     def receive(level):
         for n in range(2):
             @pl.when(inside(1 - 2 * n, 0))
             def _():
-                passing(level, n).wait_recv()
+                passing(level, n, 0).wait_recv()
+                passing(level, n, 1).wait_recv()
 
     span = range(-REACH, own + REACH - 1)
     keep(0, {r: jnp.where(lane < LANE // 2, fetch(r, width - 1), fetch(r, 0)) for r in span}, 0)
@@ -217,13 +222,14 @@
         keep(0, {r: fetch(r, q) for r in span}, q)
         return carry
 
-    lax.fori_loop(1, half + 1, first_rows, 0)
+    lax.fori_loop(1, cut, first_rows, 0)
+    send(0, 0)
+    lax.fori_loop(cut, half + 1, first_rows, 0)
+    send(0, 1)
 
     for level in range(LEVELS):
         dist = 1 << level
         trip = TRIPS[level]
-        if level < LEVELS - 1:
-            send(level)
 
         def lanes(i, carry):
             group = [
@@ -255,7 +261,12 @@
                 keep(level + 1, rows, q)
                 return carry
 
-            lax.fori_loop(0, half + 1, next_rows, 0)
+            lax.fori_loop(0, cut, next_rows, 0)
+            if level + 1 < LEVELS - 1:
+                send(level + 1, 0)
+            lax.fori_loop(cut, half + 1, next_rows, 0)
+            if level + 1 < LEVELS - 1:
+                send(level + 1, 1)
 
     copies = [
         pltpu.make_async_copy(done.at[h], out.at[:, :, pl.ds(h * half, half)], out_sem.at[h])
@@ -272,7 +283,8 @@
         for n in range(2):
             @pl.when(inside(2 * n - 1, 0))
             def _():
-                passing(level, n).wait_send()
+                passing(level, n, 0).wait_send()
+                passing(level, n, 1).wait_send()
     for copy in copies:
         copy.wait()
 
@@ -295,8 +307,8 @@
                 pltpu.VMEM((n, half + 1, 2 * images, LANE), jnp.float32)
                 for n in (REACH - 1, REACH) * (2 * (LEVELS - 1))
             ],
-            pltpu.SemaphoreType.DMA((12 + 2 * (LEVELS - 1),)),
-            pltpu.SemaphoreType.DMA((12 + 2 * (LEVELS - 1),)),
+            pltpu.SemaphoreType.DMA((12 + 4 * (LEVELS - 1),)),
+            pltpu.SemaphoreType.DMA((12 + 4 * (LEVELS - 1),)),
             pltpu.SemaphoreType.DMA((2,)),
         ],
         compiler_params=pltpu.CompilerParams(collective_id=0, has_side_effects=True, vmem_limit_bytes=40 << 20),

time: 21 us -> 20.5 us (0.976)
  Pallas kernels: 18.7 us -> 18.1 us
    pallas_call x1, Pallas kernels: 18.7 us -> 18.1 us  [shards(): pl.pallas_call(functools.partial(kernel, nr, nc), out_shape=jax.ShapeDtyp...]
where the time goes in v5:
time: 20.5 us; the launch traced here: 20.3 us
  Pallas kernels  18.1 us (88%)
  local copies, waits for them, and re-layouts  2.2 us (11%)
    pallas_call x1, Pallas kernels, shards(): pl.pallas_call(functools.partial(kernel, nr, nc), out_shape=jax.ShapeDtyp...  18.1 us
    unnamed x3, local copies, waits for them, and re-layouts  2.2 us

profile of v5, /device:TPU:9, one launch (start us, length us, event | category | flops | bytes accessed | tf_op | source)
XLA Modules:
  0.0 20.3 jit_solution(3683577368172435258)
XLA Ops:
  0.0 0.0 copy-start
  0.0 1.2 %copy-done = f32[4,32,2048]{2,1,0:T(8,128)S(1)} copy-done((f32[4,32,2048]{2,1,0:T(8,128)S(1)}, f32[4,32,2048]{2,1,0:T(8,128)}, u32[]{:S(2)}) %copy-start) | copy-done | bytes 1048600
  1.2 18.1 %shard_map.17 = f32[4,4,16,8,128]{4,3,2,1,0:T(8,128)S(1)} custom-call(f32[4,4,16,8,128]{4,3,2,1,0:T(8,128)S(1)} %bitcast.7), custom_call_target="tpu_custom_call" | custom-call | tf_op jit(solution)/shard_map/pallas_call | solution.py:297
  19.4 1.0 %copy.3 = f32[4,32,2048]{2,1,0:T(8,128)} copy(f32[4,32,2048]{2,1,0:T(8,128)S(1)} %bitcast.6) | data formatting | bytes 2097152
Async XLA Ops:
  0.0 1.2 %copy-start = (f32[4,32,2048]{2,1,0:T(8,128)S(1)}, f32[4,32,2048]{2,1,0:T(8,128)}, u32[]{:S(2)}) copy-start(f32[4,32,2048]{2,1,0:T(8,128)} %param.1) | copy-start | bytes 3145732
